TPU v7x, 32 devices: a whole 2x2x4 slice. The times are simulated.
32 devices in a mesh: row: 4 (over z), col: 8 (over y, x, core).
Axes of the slice: x: 2, y: 2, z: 4, core: 2. Of those that a mesh axis runs over, the one named last changes fastest.
Arguments:
- frontal: float32 [4096, 16384], P('row', 'col'), may hold values from -6 to 6
- sketch: float32 [16384, 256], P('col'), may hold values from -0.046875 to 0.046875
- rank_table: int32 [3, 4], replicated, may hold values from 64 to 256, as said below
Outputs:
- leaf_basis: float32 [4096, 256], P(('row', 'col'))
- top_basis: float32 [4096, 256], P(('row', 'col'))
- coupling: float32 [1024, 16384], P('row', 'col')
Inputs may be any that keep to these rules, and one draw needn't show every extreme that they name: rank_table[l, g] is the rank of the level-l node made of the 2**l consecutive row groups holding g, equal over the groups of that node; a node's rank is at most the larger of its two children's ranks; in every draw some leaf has rank 256 and some leaf rank 256 // 4.
All inputs are finite; a program needn't handle non-finite values.
Results may differ from a plain program's by a relative error of at most 0.00012.
Values sent between devices are 32-bit elements; how exact they have to be, the bound alone decides.
No kernel may reach another device: no remote copies, remote signals or barrier semaphores. Data moves between devices by JAX's collectives and lax.ppermute only.
A program may use at most 64 MiB of HBM per device.

v0:
```python
import jax
import jax.numpy as jnp
from jax import lax
from jax.sharding import PartitionSpec as P

LEVELS = 2


def swapped(block, axis, bit):
    count = lax.axis_size(axis)
    route = []
    for low in range(count):
        high = low | 1 << bit
        if high != low and high < count:
            route += [(low, high), (high, low)]
    return lax.ppermute(block, axis, route)


def product(left, right):
    return jnp.dot(left, right, precision=lax.Precision.HIGHEST, preferred_element_type=jnp.float32)


def mask_of(rank_value, width):
    return (jnp.arange(width) < rank_value).astype(jnp.float32)


def factor(gram_full, keep_mask):
    masked = keep_mask[:, None] * gram_full * keep_mask[None, :] + jnp.diag(1.0 - keep_mask)
    return jnp.linalg.cholesky(masked)


def right_solve(factor_low, operand):
    return lax.linalg.triangular_solve(
        factor_low, operand, left_side=False, lower=True, transpose_a=True
    )


def left_solve(factor_low, operand):
    return lax.linalg.triangular_solve(factor_low, operand, left_side=True, lower=True)


def body(frontal, sketch, rank_table):
    width = sketch.shape[1]
    col_count = lax.axis_size("col")
    share_rows = frontal.shape[0] // col_count
    row_group = lax.axis_index("row")
    column = lax.axis_index("col")
    keep_mask = mask_of(rank_table[0, row_group], width)
    samples = lax.psum(product(frontal, sketch), "col")
    gram_full = product(samples.T, samples)
    factor_low = factor(gram_full, keep_mask)
    full_basis = right_solve(factor_low, samples * keep_mask[None, :])
    coupling = product(full_basis.T, frontal)
    leaf_share = lax.dynamic_slice_in_dim(full_basis, column * share_rows, share_rows, 0)
    coords = left_solve(factor_low, keep_mask[:, None] * gram_full)
    chain_coef = jnp.eye(width, dtype=jnp.float32)
    for height in range(1, LEVELS + 1):
        own_gram = product(coords.T, coords)
        sibling = swapped(own_gram, "row", height - 1)
        pair_gram = own_gram + sibling
        node_mask = mask_of(rank_table[height, row_group], width)
        node_factor = factor(pair_gram, node_mask)
        chain_coef = product(chain_coef, right_solve(node_factor, coords * node_mask[None, :]))
        coords = left_solve(node_factor, node_mask[:, None] * pair_gram)
    top_share = product(leaf_share, chain_coef)
    return (leaf_share, top_share, coupling)


def solution(mesh):
    return jax.shard_map(
        body,
        mesh=mesh,
        in_specs=(P("row", "col"), P("col", None), P()),
        out_specs=(P(("row", "col"), None), P(("row", "col"), None), P("row", "col")),
        check_vma=False,
    )
```

profile of v0, /device:TPU:0, one launch (start us, length us, event | category | flops | bytes accessed | tf_op | source)
XLA Modules:
  0.0 333.1 jit_solution(14702008492156410330)
XLA Ops:
  7.2 1.5 copy-done
  8.8 10.4 %fusion.57 = f32[1024,256]{1,0:T(8,128)} fusion(f32[1024,2048]{1,0:T(8,128)} %param.8, f32[2048,256]{1,0:T(8,128)S(1)} %copy-done), kind=kOutput, calls=%fused_computation.129 | convolution fusion | flops 6442450944 | bytes 11534336 | tf_op jit(solution)/shard_map/dot_general | solution.py:20
  19.2 0.7 constant_dynamic-slice_fusion.4
  22.8 1.3 broadcast_subtract_fusion.1
  24.1 0.7 compare_convert_fusion.1
  24.8 53.9 %all-reduce.3.cloned.1.call-done = f32[1024,256]{1,0:T(8,128)} async-done(((f32[1024,256]{1,0:T(8,128)}), f32[1024,256]{1,0:T(8,128)}) %all-reduce.3.cloned.1.call-update) | async-done | bytes 1048592 | tf_op jit(solution)/shard_map/psum | solution.py:49
  78.8 4.2 %select_add_fusion.2 = (f32[256,256]{0,1:T(8,128)S(1)}, f32[256,256]{0,1:T(8,128)}) fusion(f32[256]{0:T(256)S(1)} %broadcast_subtract_fusion.2, f32[256]{0:T(256)S(1)} %compare_convert_fusion.2, f32[1024,256]{1,0:T(8,128)} %all-reduce.3.cloned.1.call-done), kind=kOutput, calls=%fused_computation.44 | convolution fusion | flops 805634048 | bytes 1574912 | tf_op jit(solution)/shard_map/dot_general | solution.py:20
  82.9 0.9 copy.7
  83.8 1.0 fusion.13
  84.8 0.7 copy-done.4
  85.5 11.7 %cholesky.172 = f32[128,128]{1,0:T(8,128)S(1)} custom-call(f32[128,128]{1,0:T(8,128)S(1)} %cholesky.270), custom_call_target="Cholesky" | custom-call | tf_op jit(solution)/shard_map/jit(cholesky)/cholesky | solution.py:29
  97.3 9.8 %custom-call.22 = f32[1,128,128]{1,2,0:T(8,128)S(1)} custom-call(f32[1,128,128]{2,1,0:T(8,128)S(1)} %get-tuple-element.98), custom_call_target="InvertDiagBlocksLowerTriangular" | custom-call | tf_op jit(solution)/shard_map/jit(cholesky)/cholesky | solution.py:29
  107.1 1.0 fusion.36
  108.2 1.1 convolution_subtract_fusion.6
  109.4 11.9 %cholesky.189 = f32[128,128]{1,0:T(8,128)S(1)} custom-call(f32[128,128]{1,0:T(8,128)S(1)} %convolution_subtract_fusion.6), custom_call_target="Cholesky" | custom-call | tf_op jit(solution)/shard_map/jit(cholesky)/cholesky | solution.py:29
  121.4 0.7 compare_reduce_fusion.4
  123.6 1.3 triangular_solve.69
  125.5 6.8 %while.9 = (s32[]{:T(128)}, f32[256,256]{0,1:T(8,128)S(1)}, s32[2,2]{1,0:T(2,128)}, f32[2,128,128]{2,1,0:T(8,128)}, s32[]{:T(128)}) while((s32[]{:T(128)}, f32[256,256]{0,1:T(8,128)S(1)}, s32[2,2]{1,0:T(2,128)}, f32[2,128,128]{2,1,0:T(8,128)}, s32[]{:T(128)}) %tuple.79), condition=%wide.while_cond.2, body=%wide.while_body.2.sunk | while | flops 2 | bytes 393329 | solution.py:33
  125.5 0.7 constant_dynamic-slice_fusion.9
  126.8 1.3 dynamic-slice.25
  128.9 0.7 constant_dynamic-slice_fusion.9
  130.2 1.3 dynamic-slice.25
  132.3 21.1 %custom-call.17 = f32[2,128,128]{1,2,0:T(8,128)} custom-call(f32[2,128,128]{2,1,0:T(8,128)} %get-tuple-element.29), custom_call_target="InvertDiagBlocksLowerTriangular" | custom-call | tf_op jit(solution)/shard_map/triangular_solve | solution.py:33
  153.4 1.3 fusion.28
  154.7 2.0 convolution_subtract_fusion.3
  156.6 0.7 copy.13
  157.4 1.2 fusion.41
  158.6 2.2 fusion.18
  160.8 1.4 collective-permute-start
  162.3 1.5 fusion.1
  163.7 1.0 convolution_subtract_fusion
  164.8 1.5 fusion.42
  166.3 0.8 copy.23
  167.0 10.7 %fusion = f32[256,2048]{1,0:T(8,128)} fusion(f32[1024,2048]{1,0:T(8,128)} %param.8, f32[1024,128]{0,1:T(8,128)S(1)} %fusion.42, f32[1024,128]{0,1:T(8,128)S(1)} %fusion.1), kind=kOutput, calls=%fused_computation.17 | convolution fusion | flops 6442713088 | bytes 11534336 | tf_op jit(solution)/shard_map/dot_general | solution.py:20
  177.8 1.2 select_add_fusion.1
  179.2 0.7 copy-done.5
  179.9 11.7 %cholesky.206 = f32[128,128]{1,0:T(8,128)S(1)} custom-call(f32[128,128]{1,0:T(8,128)S(1)} %cholesky.273), custom_call_target="Cholesky" | custom-call | tf_op jit(solution)/shard_map/jit(cholesky)/cholesky | solution.py:29
  192.3 9.8 %custom-call.24 = f32[1,128,128]{1,2,0:T(8,128)S(1)} custom-call(f32[1,128,128]{2,1,0:T(8,128)S(1)} %get-tuple-element.96), custom_call_target="InvertDiagBlocksLowerTriangular" | custom-call | tf_op jit(solution)/shard_map/jit(cholesky)/cholesky | solution.py:29
  202.1 1.0 constant_dynamic-update-slice_fusion.2
  203.1 1.1 convolution_subtract_fusion.5
  204.2 11.7 %cholesky.223 = f32[128,128]{1,0:T(8,128)S(1)} custom-call(f32[128,128]{1,0:T(8,128)S(1)} %convolution_subtract_fusion.5), custom_call_target="Cholesky" | custom-call | tf_op jit(solution)/shard_map/jit(cholesky)/cholesky | solution.py:29
  216.0 0.7 compare_reduce_fusion.2
  218.1 5.4 %while.10 = (s32[]{:T(128)}, f32[256,256]{1,0:T(8,128)S(1)}, s32[2,2]{1,0:T(2,128)}, f32[2,128,128]{2,1,0:T(8,128)S(1)}, s32[]{:T(128)}) while((s32[]{:T(128)}, f32[256,256]{1,0:T(8,128)S(1)}, s32[2,2]{1,0:T(2,128)}, f32[2,128,128]{2,1,0:T(8,128)S(1)}, s32[]{:T(128)}) %tuple.82), condition=%wide.while_cond.1, body=%wide.while_body.1.sunk | while | flops 2 | bytes 131189 | solution.py:33
  218.1 0.7 constant_dynamic-slice_fusion.10
  219.4 1.4 bitcast_dynamic-update-slice_fusion.7
  220.8 0.7 constant_dynamic-slice_fusion.10
  222.1 1.4 bitcast_dynamic-update-slice_fusion.7
  223.5 20.1 %custom-call.25 = f32[2,128,128]{1,2,0:T(8,128)S(1)} custom-call(f32[2,128,128]{2,1,0:T(8,128)S(1)} %get-tuple-element.43), custom_call_target="InvertDiagBlocksLowerTriangular" | custom-call | tf_op jit(solution)/shard_map/triangular_solve/custom-call.5 | solution.py:33
  245.7 2.5 collective-permute-start.1
  248.8 10.4 %collective-permute-done.1 = f32[256,256]{0,1:T(8,128)S(1)} collective-permute-done((f32[256,256]{0,1:T(8,128)S(1)}, f32[256,256]{0,1:T(8,128)S(1)}, u32[]{:S(2)}, u32[]{:S(2)}) %collective-permute-start.1) | collective-permute-done | bytes 262176 | tf_op jit(solution)/shard_map/ppermute | solution.py:16
  259.5 0.7 copy-done.6
  260.2 11.7 %cholesky.240 = f32[128,128]{1,0:T(8,128)S(1)} custom-call(f32[128,128]{1,0:T(8,128)S(1)} %cholesky.276), custom_call_target="Cholesky" | custom-call | tf_op jit(solution)/shard_map/jit(cholesky)/cholesky | solution.py:29
  272.6 9.8 %custom-call.27 = f32[1,128,128]{1,2,0:T(8,128)S(1)} custom-call(f32[1,128,128]{2,1,0:T(8,128)S(1)} %get-tuple-element.92), custom_call_target="InvertDiagBlocksLowerTriangular" | custom-call | tf_op jit(solution)/shard_map/jit(cholesky)/cholesky | solution.py:29
  282.4 1.0 constant_dynamic-update-slice_fusion.3
  283.5 1.1 convolution_subtract_fusion.4
  284.6 11.9 %cholesky.257 = f32[128,128]{1,0:T(8,128)S(1)} custom-call(f32[128,128]{1,0:T(8,128)S(1)} %convolution_subtract_fusion.4), custom_call_target="Cholesky" | custom-call | tf_op jit(solution)/shard_map/jit(cholesky)/cholesky | solution.py:29
  296.5 0.7 compare_reduce_fusion
  298.6 5.4 %while.11 = (s32[]{:T(128)}, f32[256,256]{1,0:T(8,128)S(1)}, s32[2,2]{1,0:T(2,128)}, f32[2,128,128]{2,1,0:T(8,128)S(1)}, s32[]{:T(128)}) while((s32[]{:T(128)}, f32[256,256]{1,0:T(8,128)S(1)}, s32[2,2]{1,0:T(2,128)}, f32[2,128,128]{2,1,0:T(8,128)S(1)}, s32[]{:T(128)}) %tuple.85), condition=%wide.while_cond.1.clone, body=%wide.while_body.1.clone.sunk | while | flops 2 | bytes 131189 | solution.py:33
  298.6 0.7 constant_dynamic-slice_fusion.11
  299.8 1.4 bitcast_dynamic-update-slice_fusion.8
  301.3 0.7 constant_dynamic-slice_fusion.11
  302.5 1.4 bitcast_dynamic-update-slice_fusion.8
  304.0 19.7 %custom-call.28 = f32[2,128,128]{1,2,0:T(8,128)S(1)} custom-call(f32[2,128,128]{2,1,0:T(8,128)S(1)} %get-tuple-element.45), custom_call_target="InvertDiagBlocksLowerTriangular" | custom-call | tf_op jit(solution)/shard_map/triangular_solve/custom-call.5 | solution.py:33
  325.0 1.1 fusion.58
  (77 shorter events, 15.4 us)
Async XLA Ops:
  7.2 1.6 copy-start
  7.2 12.0 %copy-start.7 = (s32[3,4]{1,0:T(4,128)S(1)}, s32[3,4]{1,0:T(4,128)}, u32[]{:S(2)}) copy-start(s32[3,4]{1,0:T(4,128)} %param.10) | copy-start | bytes 148
  7.2 71.6 %all-reduce.3.cloned.1.call-start = ((), (), s32[]{:S(2)}) async-start(), calls=%async_computation | async-start | bytes 2097152 | tf_op jit(solution)/shard_map/psum | solution.py:49
  78.8 83.4 %copy-start.1 = (f32[1024,256]{1,0:T(8,128)S(1)}, f32[1024,256]{1,0:T(8,128)}, u32[]{:S(2)}) copy-start(f32[1024,256]{1,0:T(8,128)} %all-reduce.3.cloned.1.call-done) | copy-start | bytes 3145732
  84.7 0.7 copy-start.4
  158.6 6.1 %copy-start.2 = (f32[128,256]{0,1:T(8,128)}, f32[128,256]{0,1:T(8,128)S(1)}, u32[]{:S(2)}) copy-start(f32[128,256]{0,1:T(8,128)S(1)} %fusion.41) | copy-start | bytes 393220
  160.8 17.0 %collective-permute-start = (f32[256,256]{0,1:T(8,128)}, f32[256,256]{0,1:T(8,128)}, u32[]{:S(2)}, u32[]{:S(2)}) collective-permute-start(f32[256,256]{0,1:T(8,128)} %fusion.18), channel_id=1, source_target_pairs={{0,8},{8,0},{16,24},{24,16},{1,9},{9,1},{17,25},{25,17},{2,10},{10... | collective-permute-start | bytes 786440 | tf_op jit(solution)/shard_map/ppermute | solution.py:16
  162.3 15.5 %copy-start.8 = (f32[256]{0:T(256)S(1)}, f32[256]{0:T(256)}, u32[]{:S(2)}) copy-start(f32[256]{0:T(256)} %broadcast_subtract_fusion.1) | copy-start | bytes 3076
  166.2 11.6 %copy-start.3 = (f32[128,256]{0,1:T(8,128)S(1)}, f32[128,256]{0,1:T(8,128)}, u32[]{:S(2)}) copy-start(f32[128,256]{0,1:T(8,128)} %copy-done.2) | copy-start | bytes 393220
  179.2 0.7 copy-start.5
  245.7 13.5 %collective-permute-start.1 = (f32[256,256]{0,1:T(8,128)S(1)}, f32[256,256]{0,1:T(8,128)S(1)}, u32[]{:S(2)}, u32[]{:S(2)}) collective-permute-start(f32[256,256]{0,1:T(8,128)S(1)} %fusion.16), channel_id=1, source_target_pairs={{0,16},{16,0},{8,24},{24,8},{1,17},{17,1},{9,25},{25,9},{2,18},{18... | collective-permute-start | bytes 786440 | tf_op jit(solution)/shard_map/ppermute | solution.py:16
  259.5 0.7 copy-start.6
Sparse Core Ops, SparseCore 0:
  19.3 59.4 all-reduce.2
where the time goes:
time: 337 us; the launch traced here: 333 us
  other arithmetic  172 us (51%)
  waiting for transfers between devices  64.3 us (19%)
  matrix products  47.1 us (14%)
  local copies, waits for them, and re-layouts  26.8 us (8%)
  between operations  18.8 us (6%)
  starting transfers between devices  3.94 us (1%)
    another operation x20, other arithmetic, factor(): return jnp.linalg.cholesky(masked)  104 us
    another operation x8, other arithmetic, right_solve(): lax.linalg.triangular_solve(factor_low, operand, left_side=False, lower=T...  61.5 us
    psum x1, waiting for transfers between devices, body(): samples = lax.psum(product(frontal, sketch), 'col')  53.9 us
    dot_general x8, matrix products, product(): jnp.dot(left, right, precision=lax.Precision.HIGHEST, preferred_element_t...  29.6 us
    another operation x13, local copies, waits for them, and re-layouts, right_solve(): lax.linalg.triangular_solve(factor_low, operand, left_side=False, lower=T...  12 us
    ppermute x2, waiting for transfers between devices, swapped(): return lax.ppermute(block, axis, route)  10.4 us
    another operation x10, local copies, waits for them, and re-layouts  6.8 us
  transfers between devices with their start and end apart: 3, of which 2 were waited for; matrix products, arithmetic and copies ran while one was open for 7% of the time, Pallas kernels for 0%

commit v1 on v0

v1 whole, which is shorter than its diff:
```python
import functools

import jax
import jax.numpy as jnp
from jax import lax
from jax.experimental import pallas as pl
from jax.experimental.pallas import tpu as pltpu
from jax.sharding import PartitionSpec as P

LEVELS = 2
TILE = 8
BLOCK = 64
F32 = jnp.float32
BF16 = jnp.bfloat16
EXACT = lax.Precision.HIGHEST
VMEM = pl.BlockSpec(memory_space=pltpu.VMEM)
SMEM = pl.BlockSpec(memory_space=pltpu.SMEM)


def contract(left, right, dim_left, dim_right, precision=None):
    return lax.dot_general(
        left, right, (((dim_left,), (dim_right,)), ((), ())), precision=precision, preferred_element_type=F32
    )


def halves(value):
    high = value.astype(BF16)
    return high, (value - high.astype(F32)).astype(BF16)


def contract3(left, right, dim_left, dim_right):
    (lh, ll), (rh, rl) = left, right
    return (
        contract(lh, rh, dim_left, dim_right)
        + contract(lh, rl, dim_left, dim_right)
        + contract(ll, rh, dim_left, dim_right)
    )


def eye_like(shape):
    rows = lax.broadcasted_iota(jnp.int32, shape, 0)
    cols = lax.broadcasted_iota(jnp.int32, shape, 1)
    return (rows == cols).astype(F32)


def over_lanes(tile, lane):
    return jnp.broadcast_to(tile[:, lane : lane + 1], tile.shape)


def over_rows(tile, row):
    return jnp.broadcast_to(tile[row : row + 1, :], tile.shape)


def small_inverse_factor(block):
    n = block.shape[0]
    wide = jnp.concatenate([block, eye_like((n, n))], axis=1)
    work = [wide[TILE * t : TILE * (t + 1)] for t in range(n // TILE)]
    row_of = lax.broadcasted_iota(jnp.int32, work[0].shape, 0)
    out = []
    for t in range(len(work)):
        cols = {u: [over_lanes(work[u], TILE * t + k) for k in range(TILE)] for u in range(t, len(work))}
        pivots = None
        for j in range(TILE):
            across = [over_rows(cols[t][k], j) if k >= j else None for k in range(TILE)]
            pivot = across[j]
            scale = 1.0 / pivot
            pivot_row = over_rows(work[t], j)
            pivots = pivot if pivots is None else jnp.where(row_of == j, pivot, pivots)
            for u in range(t, len(work)):
                step = cols[u][j] * scale
                if u == t:
                    step = jnp.where(row_of > j, step, 0.0)
                for k in range(j + 1, TILE):
                    cols[u][k] = cols[u][k] - step * across[k]
                work[u] = work[u] - step * pivot_row
        out.append(work[t] * lax.rsqrt(pivots))
    return jnp.concatenate(out, axis=0)[:, n:]


def masked_inverse_factor(gram, rank, s_ref, p_ref):
    n = gram.shape[0]
    rows = lax.broadcasted_iota(jnp.int32, (n, n), 0)
    cols = lax.broadcasted_iota(jnp.int32, (n, n), 1)
    s_ref[...] = jnp.where((rows < rank) & (cols < rank), gram, (rows == cols).astype(F32))
    p_ref[...] = (rows == cols).astype(F32)
    for low in range(0, n, BLOCK):
        high = low + BLOCK
        inverse = small_inverse_factor(s_ref[low:high, low:high])
        extra = contract(inverse, p_ref[low:high, :], 1, 0, EXACT)
        p_ref[low:high, :] = extra
        if high < n:
            panel = contract(inverse, s_ref[low:high, :], 1, 0, EXACT)
            s_ref[high:, :] = s_ref[high:, :] - contract(panel[:, high:], panel, 0, 0, EXACT)
            p_ref[high:, :] = p_ref[high:, :] - contract(panel[:, high:], extra, 0, 0, EXACT)
    p_ref[...] = jnp.where(rows < rank, p_ref[...], 0.0)


def samples_kernel(index_ref, frontal_ref, sketch_ref, out_ref, high_ref, low_ref):
    @pl.when(pl.program_id(0) == 0)
    def _():
        high_ref[...], low_ref[...] = halves(sketch_ref[...])

    out_ref[...] = contract3(halves(frontal_ref[...]), (high_ref[...], low_ref[...]), 1, 0)


def partial_samples(index, frontal, sketch, parts, offset):
    share = frontal.shape[0] // parts
    inner, width = sketch.shape
    return pl.pallas_call(
        samples_kernel,
        grid_spec=pltpu.PrefetchScalarGridSpec(
            num_scalar_prefetch=1,
            grid=(parts // 2,),
            in_specs=[
                pl.BlockSpec((share, inner), lambda d, index: (index[0] ^ (2 * d + offset), 0)),
                pl.BlockSpec((inner, width), lambda d, index: (0, 0)),
            ],
            out_specs=pl.BlockSpec((share, width), lambda d, index: (d, 0)),
            scratch_shapes=[pltpu.VMEM((inner, width), BF16)] * 2,
        ),
        out_shape=jax.ShapeDtypeStruct((frontal.shape[0] // 2, width), F32),
        name="partial_samples",
    )(index, frontal, sketch)


def leaf_kernel(rank_ref, *refs):
    pieces, (p_ref, coords_ref, own_ref, s_ref) = refs[:-4], refs[-4:]
    gram = None
    for piece in pieces:
        part = halves(piece[...])
        term = contract3(part, part, 0, 0)
        gram = term if gram is None else gram + term
    masked_inverse_factor(gram, rank_ref[0], s_ref, p_ref)
    coords = contract(p_ref[...], gram, 1, 0, EXACT)
    coords_ref[...] = coords
    own_ref[...] = contract(coords, coords, 0, 0, EXACT)


def leaf_factor(rank, pieces):
    width = pieces[0].shape[1]
    square = jax.ShapeDtypeStruct((width, width), F32)
    return pl.pallas_call(
        leaf_kernel,
        in_specs=[SMEM] + [VMEM] * len(pieces),
        out_specs=(VMEM,) * 3,
        out_shape=(square,) * 3,
        scratch_shapes=[pltpu.VMEM((width, width), F32)],
        name="leaf_factor",
    )(rank, *pieces)


def coupling_kernel(count, index_ref, p_ref, frontal_ref, *refs):
    pieces, (share_ref, out_ref, high_ref, low_ref) = refs[:count], refs[count:]
    share = pieces[0].shape[0]

    @pl.when(pl.program_id(0) == 0)
    def _():
        inverse = halves(p_ref[...])
        for at, piece in enumerate(pieces):
            basis = contract3(halves(piece[...]), inverse, 1, 1)
            if at == 0:
                share_ref[...] = basis
            start = pl.multiple_of((index_ref[0] ^ at) * share, share)
            high_ref[pl.ds(start, share), :], low_ref[pl.ds(start, share), :] = halves(basis)

    out_ref[...] = contract3((high_ref[...], low_ref[...]), halves(frontal_ref[...]), 0, 0)


def couplings(index, inverse, frontal, pieces, blocks=4):
    rows, cols = frontal.shape
    share, width = pieces[0].shape
    return pl.pallas_call(
        functools.partial(coupling_kernel, len(pieces)),
        grid_spec=pltpu.PrefetchScalarGridSpec(
            num_scalar_prefetch=1,
            grid=(blocks,),
            in_specs=[
                pl.BlockSpec((width, width), lambda b, index: (0, 0)),
                pl.BlockSpec((rows, cols // blocks), lambda b, index: (0, b)),
            ]
            + [pl.BlockSpec((share, width), lambda b, index: (0, 0))] * len(pieces),
            out_specs=(
                pl.BlockSpec((share, width), lambda b, index: (0, 0)),
                pl.BlockSpec((width, cols // blocks), lambda b, index: (0, b)),
            ),
            scratch_shapes=[pltpu.VMEM((rows, width), BF16)] * 2,
        ),
        out_shape=(jax.ShapeDtypeStruct((share, width), F32), jax.ShapeDtypeStruct((width, cols), F32)),
        name="couplings",
    )(index, inverse, frontal, *pieces)


def node_kernel(rank_ref, own_ref, sibling_ref, coords_ref, top_ref, next_own_ref, next_coords_ref, next_top_ref, s_ref, p_ref):
    pair = own_ref[...] + sibling_ref[...]
    masked_inverse_factor(pair, rank_ref[0], s_ref, p_ref)
    inverse = p_ref[...]
    upper = contract(inverse, pair, 1, 0, EXACT)
    next_coords_ref[...] = upper
    next_own_ref[...] = contract(upper, upper, 0, 0, EXACT)
    carried = contract(top_ref[...], coords_ref[...], 1, 0, EXACT)
    next_top_ref[...] = contract(carried, inverse, 1, 1, EXACT)


def node(rank, own, sibling, coords, top):
    width = own.shape[0]
    square = jax.ShapeDtypeStruct((width, width), F32)
    return pl.pallas_call(
        node_kernel,
        in_specs=[SMEM] + [VMEM] * 4,
        out_specs=(VMEM,) * 3,
        out_shape=(square, square, jax.ShapeDtypeStruct(top.shape, F32)),
        scratch_shapes=[pltpu.VMEM((width, width), F32)] * 2,
        name="node",
    )(rank, own, sibling, coords, top)


def swapped(block, axis, distance):
    count = lax.axis_size(axis)
    route = [(low, low ^ distance) for low in range(count) if low ^ distance < count]
    return lax.ppermute(block, axis, route)


def body(frontal, sketch, rank_table):
    parts = lax.axis_size("col")
    chips = parts // 2
    share = frontal.shape[0] // parts
    row_group = lax.axis_index("row")
    index = lax.axis_index("col").astype(jnp.int32).reshape(1)
    ranks = lax.dynamic_slice_in_dim(rank_table, row_group, 1, 1)

    leaving = partial_samples(index, frontal, sketch, parts, 1)
    arriving = swapped(leaving, "col", 1)
    staying = partial_samples(index, frontal, sketch, parts, 0)
    chip_sum = staying + arriving
    part_of = lambda at: chip_sum[at * share : (at + 1) * share]
    total = part_of(0)
    for other in [swapped(part_of(at), "col", 2 * at) for at in range(1, chips)]:
        total = total + other
    gathered = [total] + [swapped(total, "col", 2 * at) for at in range(1, chips)]
    pieces = []
    for piece in gathered:
        pieces += [piece, swapped(piece, "col", 1)]

    inverse, coords, own = leaf_factor(ranks[0], pieces)
    sibling = swapped(own, "row", 1)
    leaf_share, coupling = couplings(index, inverse, frontal, pieces)
    top = leaf_share
    for height in range(1, LEVELS + 1):
        if height > 1:
            sibling = swapped(own, "row", 1 << (height - 1))
        own, coords, top = node(ranks[height], own, sibling, coords, top)
    return (leaf_share, top, coupling)


def solution(mesh):
    return jax.shard_map(
        body,
        mesh=mesh,
        in_specs=(P("row", "col"), P("col", None), P()),
        out_specs=(P(("row", "col"), None), P(("row", "col"), None), P("row", "col")),
        check_vma=False,
    )
```

time: 337 us -> 105 us (0.31); the launches traced: 333 us -> 105 us
  other arithmetic: 172 us -> 1.17 us
  Pallas kernels: 0 us -> 63.1 us
  matrix products: 47.1 us -> 0 us
  waiting for transfers between devices: 64.3 us -> 24.6 us
  local copies, waits for them, and re-layouts: 26.8 us -> 2.74 us
  between operations: 18.8 us -> 0.72 us
  starting transfers between devices: 3.94 us -> 12.8 us
    another operation x28 -> x0, other arithmetic: 165 us -> none  [the longest x20 104 us: factor(): return jnp.linalg.cholesky(masked)]
    pallas_call x0 -> x6, Pallas kernels: none -> 63.1 us  [the longest x2 26.9 us: node(): pl.pallas_call(node_kernel, in_specs=[SMEM] + [VMEM] * 4, out_specs=(VMEM...]
    psum x1 -> x0, waiting for transfers between devices: 53.9 us -> none  [body(): samples = lax.psum(product(frontal, sketch), 'col')]
    dot_general x8 -> x0, matrix products: 29.6 us -> none  [product(): jnp.dot(left, right, precision=lax.Precision.HIGHEST, preferred_element_t...]
    another operation x36 -> x0, local copies, waits for them, and re-layouts: 20 us -> none  [the longest x13 12 us: right_solve(): lax.linalg.triangular_solve(factor_low, operand, left_side=False, lower=T...]
    another operation x21 -> x0, matrix products: 17.5 us -> none  [the longest x6 6.44 us: factor(): return jnp.linalg.cholesky(masked)]
    ppermute x2 -> x13, waiting for transfers between devices: 10.4 us -> 24.6 us  [swapped(): return lax.ppermute(block, axis, route)]
    ppermute x2 -> x13, starting transfers between devices: 3.9 us -> 12.8 us  [swapped(): return lax.ppermute(block, axis, route)]
  transfers between devices with their start and end apart: 3 -> 13, of which waited for: 2 -> 8; matrix products, arithmetic and copies ran while one was open for 7% -> 1% of each run, Pallas kernels for 0% -> 14%
where the time goes in v1:
time: 105 us
  Pallas kernels  63.1 us (60%)
  waiting for transfers between devices  24.6 us (23%)
  starting transfers between devices  12.8 us (12%)
  local copies, waits for them, and re-layouts  2.74 us (3%)
  other arithmetic  1.17 us (1%)
    pallas_call x2, Pallas kernels, node(): pl.pallas_call(node_kernel, in_specs=[SMEM] + [VMEM] * 4, out_specs=(VMEM...  26.9 us
    ppermute x13, waiting for transfers between devices, swapped(): return lax.ppermute(block, axis, route)  24.6 us
    pallas_call x1, Pallas kernels, leaf_factor(): pl.pallas_call(leaf_kernel, in_specs=[SMEM] + [VMEM] * len(pieces), out_s...  15.2 us
    ppermute x13, starting transfers between devices, swapped(): return lax.ppermute(block, axis, route)  12.8 us
    pallas_call x2, Pallas kernels, partial_samples(): pl.pallas_call(samples_kernel, grid_spec=pltpu.PrefetchScalarGridSpec(num...  12 us
    pallas_call x1, Pallas kernels, couplings(): pl.pallas_call(functools.partial(coupling_kernel, len(pieces)), grid_spec...  8.9 us
  transfers between devices with their start and end apart: 13, of which 8 were waited for; matrix products, arithmetic and copies ran while one was open for 1% of the time, Pallas kernels for 14%

profile of v1, /device:TPU:0, one launch (start us, length us, event | category | flops | bytes accessed | tf_op | source)
XLA Modules:
  0.0 105.1 jit_solution(1025608085305709551)
XLA Ops:
  0.6 0.0 copy-start
  0.7 6.0 %partial_samples.3 = f32[512,256]{1,0:T(8,128)} custom-call(s32[1]{0:T(128)} %bitcast.index_ref, f32[1024,2048]{1,0:T(8,128)} %frontal_ref.5, f32[2048,256]{1,0:T(8,128)} %sketch_ref.3), custom_call_target="tpu_custom_call" | custom-call | tf_op jit(solution)/shard_map/partial_samples/pallas_call | solution.py:109
  6.7 0.5 collective-permute-start
  7.2 6.0 %partial_samples.2 = f32[512,256]{1,0:T(8,128)} custom-call(s32[1]{0:T(128)} %bitcast.index_ref, f32[1024,2048]{1,0:T(8,128)} %frontal_ref.5, f32[2048,256]{1,0:T(8,128)} %sketch_ref.3), custom_call_target="tpu_custom_call" | custom-call | tf_op jit(solution)/shard_map/partial_samples/pallas_call | solution.py:109
  13.2 0.0 collective-permute-done
  13.2 1.1 %add.16 = f32[512,256]{1,0:T(8,128)S(1)} add(f32[512,256]{1,0:T(8,128)} %partial_samples.2, f32[512,256]{1,0:T(8,128)S(1)} %collective-permute-done) | non-fusion elementwise | flops 131072 | bytes 1572864 | tf_op jit(solution)/shard_map/add | solution.py:234
  14.4 2.6 %collective-permute-start.1 = (f32[128,256]{1,0:T(8,128)S(1)}, f32[128,256]{1,0:T(8,128)S(1)}, u32[]{:S(2)}, u32[]{:S(2)}) collective-permute-start(f32[128,256]{1,0:T(8,128)S(1)} %get-tuple-element.21), channel_id=1, source_target_pairs={{0,2},{1,3},{2,0},{3,1},{4,6},{5,7},{6,4},{7,5},{8,10},{9,11},{10,... | collective-permute-start | bytes 393224 | tf_op jit(solution)/shard_map/ppermute | solution.py:220
  16.9 1.5 %collective-permute-start.2 = (f32[128,256]{1,0:T(8,128)S(1)}, f32[128,256]{1,0:T(8,128)S(1)}, u32[]{:S(2)}, u32[]{:S(2)}) collective-permute-start(f32[128,256]{1,0:T(8,128)S(1)} %get-tuple-element.23), channel_id=1, source_target_pairs={{0,4},{1,5},{2,6},{3,7},{4,0},{5,1},{6,2},{7,3},{8,12},{9,13},{10,... | collective-permute-start | bytes 393224 | tf_op jit(solution)/shard_map/ppermute | solution.py:220
  18.4 0.0 collective-permute-start.3
  18.5 2.8 %collective-permute-done.1 = f32[128,256]{1,0:T(8,128)S(1)} collective-permute-done((f32[128,256]{1,0:T(8,128)S(1)}, f32[128,256]{1,0:T(8,128)S(1)}, u32[]{:S(2)}, u32[]{:S(2)}) %collective-permute-start.1) | collective-permute-done | bytes 131104 | tf_op jit(solution)/shard_map/ppermute | solution.py:220
  21.2 4.1 %collective-permute-done.2 = f32[128,256]{1,0:T(8,128)S(1)} collective-permute-done((f32[128,256]{1,0:T(8,128)S(1)}, f32[128,256]{1,0:T(8,128)S(1)}, u32[]{:S(2)}, u32[]{:S(2)}) %collective-permute-start.2) | collective-permute-done | bytes 131104 | tf_op jit(solution)/shard_map/ppermute | solution.py:220
  25.3 0.0 collective-permute-done.3
  25.4 0.0 copy-start.1
  25.4 1.6 %collective-permute-start.9 = (f32[128,256]{1,0:T(8,128)S(1)}, f32[128,256]{1,0:T(8,128)S(1)}, u32[]{:S(2)}, u32[]{:S(2)}) collective-permute-start(f32[128,256]{1,0:T(8,128)S(1)} %fusion.1.refs_0_), channel_id=1, source_target_pairs={{0,6},{1,7},{2,4},{3,5},{4,2},{5,3},{6,0},{7,1},{8,14},{9,15},{10,... | collective-permute-start | bytes 393224 | tf_op jit(solution)/shard_map/ppermute | solution.py:220
  26.9 1.5 %collective-permute-start.5 = (f32[128,256]{1,0:T(8,128)S(1)}, f32[128,256]{1,0:T(8,128)S(1)}, u32[]{:S(2)}, u32[]{:S(2)}) collective-permute-start(f32[128,256]{1,0:T(8,128)S(1)} %fusion.1.refs_0_), channel_id=1, source_target_pairs={{0,2},{1,3},{2,0},{3,1},{4,6},{5,7},{6,4},{7,5},{8,10},{9,11},{10,... | collective-permute-start | bytes 393224 | tf_op jit(solution)/shard_map/ppermute | solution.py:220
  28.4 0.5 collective-permute-start.7
  28.9 0.0 collective-permute-start.4
  28.9 3.6 %collective-permute-done.9.refs_6_ = f32[128,256]{1,0:T(8,128)S(1)} collective-permute-done((f32[128,256]{1,0:T(8,128)S(1)}, f32[128,256]{1,0:T(8,128)S(1)}, u32[]{:S(2)}, u32[]{:S(2)}) %collective-permute-start.9) | collective-permute-done | bytes 131104 | tf_op jit(solution)/shard_map/ppermute | solution.py:220
  32.5 0.0 copy-start.2
  32.5 0.0 collective-permute-start.10
  32.5 1.4 %collective-permute-done.5.refs_2_ = f32[128,256]{1,0:T(8,128)S(1)} collective-permute-done((f32[128,256]{1,0:T(8,128)S(1)}, f32[128,256]{1,0:T(8,128)S(1)}, u32[]{:S(2)}, u32[]{:S(2)}) %collective-permute-start.5) | collective-permute-done | bytes 131104 | tf_op jit(solution)/shard_map/ppermute | solution.py:220
  34.0 0.0 copy-start.3
  34.0 0.0 collective-permute-start.6
  34.0 0.1 collective-permute-done.7.refs_4_
  34.0 0.0 copy-start.4
  34.0 0.5 collective-permute-start.8
  34.5 0.0 copy-done
  34.5 0.1 constant_dynamic-slice_fusion
  34.6 0.6 fusion.3
  35.2 0.0 collective-permute-done.4.refs_1_
  35.2 0.0 copy-start.5
  35.2 0.0 collective-permute-done.10.refs_7_
  35.2 0.0 copy-start.6
  35.2 0.1 collective-permute-done.6.refs_3_
  35.3 0.0 copy-start.7
  35.3 0.2 collective-permute-done.8.refs_5_
  35.5 0.0 copy-start.8
  35.5 0.0 copy-done.1
  35.5 0.0 copy-done.2
  35.5 0.0 copy-done.3
  35.5 0.0 copy-done.4
  35.5 0.3 copy-done.5
  35.8 0.0 copy-done.6
  35.9 0.1 copy-done.7
  36.0 0.2 copy-done.8
  36.2 15.2 %leaf_factor.1 = (f32[256,256]{1,0:T(8,128)}, f32[256,256]{1,0:T(8,128)}, f32[256,256]{1,0:T(8,128)}) custom-call(s32[1]{0:T(128)} %bitcast.1.rank_ref, f32[128,256]{1,0:T(8,128)} %copy-done.1, f32[128,256]{1,0:T(8,128)} %copy-done.5, f32[128,256]{1,0:T(8,128)} %copy-done.3, f32[128,256]{1,0:T(8,128)} %copy-done.7, f32[128,256]{1,0:T(8,128)} %copy-done.4, ...), custom_call_target="tpu_custom_call" | custom-call | tf_op jit(solution)/shard_map/leaf_factor/pallas_call | solution.py:142
  51.4 1.6 %collective-permute-start.11 = (f32[256,256]{1,0:T(8,128)}, f32[256,256]{1,0:T(8,128)S(1)}, u32[]{:S(2)}, u32[]{:S(2)}) collective-permute-start(f32[256,256]{1,0:T(8,128)} %get-tuple-element.14.own_ref), channel_id=1, source_target_pairs={{0,8},{8,0},{16,24},{24,16},{1,9},{9,1},{17,25},{25,17},{2,10},{10... | collective-permute-start | bytes 786440 | tf_op jit(solution)/shard_map/ppermute | solution.py:220
  52.9 8.9 %couplings.1 = (f32[128,256]{1,0:T(8,128)}, f32[256,2048]{1,0:T(8,128)}) custom-call(s32[1]{0:T(128)} %bitcast.index_ref, f32[256,256]{1,0:T(8,128)} %get-tuple-element.12.p_ref, f32[1024,2048]{1,0:T(8,128)} %frontal_ref.5, f32[128,256]{1,0:T(8,128)} %copy-done.1, f32[128,256]{1,0:T(8,128)} %copy-done.5, f32[128,256]{1,0:T(8,128)} %copy-done.3, ...), custom_call_target="tpu_custom_call" | custom-call | tf_op jit(solution)/shard_map/couplings/pallas_call | solution.py:172
  61.8 0.0 collective-permute-done.11.sibling_ref
  61.8 0.0 copy-start.9
  61.9 0.7 copy-done.9
  62.5 13.5 %node.2 = (f32[256,256]{1,0:T(8,128)}, f32[256,256]{1,0:T(8,128)}, f32[128,256]{1,0:T(8,128)}) custom-call(s32[1]{0:T(128)} %bitcast.3.rank_ref, f32[256,256]{1,0:T(8,128)} %get-tuple-element.14.own_ref, f32[256,256]{1,0:T(8,128)} %copy-done.9, f32[256,256]{1,0:T(8,128)} %get-tuple-element.15.coords_ref, f32[128,256]{1,0:T(8,128)} %get-tuple-element.9.top_ref), custom_call_target="tpu_custom_call" | custom-call | tf_op jit(solution)/shard_map/node/pallas_call | solution.py:207
  76.1 2.6 %collective-permute-start.12 = (f32[256,256]{1,0:T(8,128)}, f32[256,256]{1,0:T(8,128)S(1)}, u32[]{:S(2)}, u32[]{:S(2)}) collective-permute-start(f32[256,256]{1,0:T(8,128)} %get-tuple-element.16.own_ref), channel_id=1, source_target_pairs={{0,16},{8,24},{16,0},{24,8},{1,17},{9,25},{17,1},{25,9},{2,18},{10... | collective-permute-start | bytes 786440 | tf_op jit(solution)/shard_map/ppermute | solution.py:220
  78.7 12.3 %collective-permute-done.12.sibling_ref = f32[256,256]{1,0:T(8,128)S(1)} collective-permute-done((f32[256,256]{1,0:T(8,128)}, f32[256,256]{1,0:T(8,128)S(1)}, u32[]{:S(2)}, u32[]{:S(2)}) %collective-permute-start.12) | collective-permute-done | bytes 262176 | tf_op jit(solution)/shard_map/ppermute | solution.py:220
  91.0 0.0 copy-start.10
  91.0 0.7 copy-done.10
  91.7 13.4 %node.3 = (f32[256,256]{1,0:T(8,128)}, f32[256,256]{1,0:T(8,128)}, f32[128,256]{1,0:T(8,128)}) custom-call(s32[1]{0:T(128)} %bitcast.2.rank_ref, f32[256,256]{1,0:T(8,128)} %get-tuple-element.16.own_ref, f32[256,256]{1,0:T(8,128)} %copy-done.10, f32[256,256]{1,0:T(8,128)} %get-tuple-element.17.coords_ref, f32[128,256]{1,0:T(8,128)} %get-tuple-element.18.top_ref), custom_call_target="tpu_custom_call" | custom-call | tf_op jit(solution)/shard_map/node/pallas_call | solution.py:207
  (2 shorter events, 0.1 us)
Async XLA Ops:
  0.6 33.9 %copy-start = (s32[3,4]{1,0:T(4,128)S(1)}, s32[3,4]{1,0:T(4,128)}, u32[]{:S(2)}) copy-start(s32[3,4]{1,0:T(4,128)} %param.5) | copy-start | bytes 148
  6.7 6.5 %collective-permute-start = (f32[512,256]{1,0:T(8,128)}, f32[512,256]{1,0:T(8,128)S(1)}, u32[]{:S(2)}, u32[]{:S(2)}) collective-permute-start(f32[512,256]{1,0:T(8,128)} %partial_samples.3), channel_id=1, source_target_pairs={{0,1},{1,0},{2,3},{3,2},{4,5},{5,4},{6,7},{7,6},{8,9},{9,8},{10,11... | collective-permute-start | bytes 1572872 | tf_op jit(solution)/shard_map/ppermute | solution.py:220
  14.4 6.9 %collective-permute-start.1 = (f32[128,256]{1,0:T(8,128)S(1)}, f32[128,256]{1,0:T(8,128)S(1)}, u32[]{:S(2)}, u32[]{:S(2)}) collective-permute-start(f32[128,256]{1,0:T(8,128)S(1)} %get-tuple-element.21), channel_id=1, source_target_pairs={{0,2},{1,3},{2,0},{3,1},{4,6},{5,7},{6,4},{7,5},{8,10},{9,11},{10,... | collective-permute-start | bytes 393224 | tf_op jit(solution)/shard_map/ppermute | solution.py:220
  16.9 8.4 %collective-permute-start.2 = (f32[128,256]{1,0:T(8,128)S(1)}, f32[128,256]{1,0:T(8,128)S(1)}, u32[]{:S(2)}, u32[]{:S(2)}) collective-permute-start(f32[128,256]{1,0:T(8,128)S(1)} %get-tuple-element.23), channel_id=1, source_target_pairs={{0,4},{1,5},{2,6},{3,7},{4,0},{5,1},{6,2},{7,3},{8,12},{9,13},{10,... | collective-permute-start | bytes 393224 | tf_op jit(solution)/shard_map/ppermute | solution.py:220
  18.4 6.9 %collective-permute-start.3 = (f32[128,256]{1,0:T(8,128)S(1)}, f32[128,256]{1,0:T(8,128)S(1)}, u32[]{:S(2)}, u32[]{:S(2)}) collective-permute-start(f32[128,256]{1,0:T(8,128)S(1)} %get-tuple-element.22), channel_id=1, source_target_pairs={{0,6},{1,7},{2,4},{3,5},{4,2},{5,3},{6,0},{7,1},{8,14},{9,15},{10,... | collective-permute-start | bytes 393224 | tf_op jit(solution)/shard_map/ppermute | solution.py:220
  25.4 10.1 %copy-start.1 = (f32[128,256]{1,0:T(8,128)}, f32[128,256]{1,0:T(8,128)S(1)}, u32[]{:S(2)}) copy-start(f32[128,256]{1,0:T(8,128)S(1)} %fusion.1.refs_0_) | copy-start | bytes 393220
  25.4 7.1 %collective-permute-start.9 = (f32[128,256]{1,0:T(8,128)S(1)}, f32[128,256]{1,0:T(8,128)S(1)}, u32[]{:S(2)}, u32[]{:S(2)}) collective-permute-start(f32[128,256]{1,0:T(8,128)S(1)} %fusion.1.refs_0_), channel_id=1, source_target_pairs={{0,6},{1,7},{2,4},{3,5},{4,2},{5,3},{6,0},{7,1},{8,14},{9,15},{10,... | collective-permute-start | bytes 393224 | tf_op jit(solution)/shard_map/ppermute | solution.py:220
  26.9 7.0 %collective-permute-start.5 = (f32[128,256]{1,0:T(8,128)S(1)}, f32[128,256]{1,0:T(8,128)S(1)}, u32[]{:S(2)}, u32[]{:S(2)}) collective-permute-start(f32[128,256]{1,0:T(8,128)S(1)} %fusion.1.refs_0_), channel_id=1, source_target_pairs={{0,2},{1,3},{2,0},{3,1},{4,6},{5,7},{6,4},{7,5},{8,10},{9,11},{10,... | collective-permute-start | bytes 393224 | tf_op jit(solution)/shard_map/ppermute | solution.py:220
  28.4 5.6 %collective-permute-start.7 = (f32[128,256]{1,0:T(8,128)S(1)}, f32[128,256]{1,0:T(8,128)S(1)}, u32[]{:S(2)}, u32[]{:S(2)}) collective-permute-start(f32[128,256]{1,0:T(8,128)S(1)} %fusion.1.refs_0_), channel_id=1, source_target_pairs={{0,4},{1,5},{2,6},{3,7},{4,0},{5,1},{6,2},{7,3},{8,12},{9,13},{10,... | collective-permute-start | bytes 393224 | tf_op jit(solution)/shard_map/ppermute | solution.py:220
  28.9 6.2 %collective-permute-start.4 = (f32[128,256]{1,0:T(8,128)S(1)}, f32[128,256]{1,0:T(8,128)S(1)}, u32[]{:S(2)}, u32[]{:S(2)}) collective-permute-start(f32[128,256]{1,0:T(8,128)S(1)} %fusion.1.refs_0_), channel_id=1, source_target_pairs={{0,1},{1,0},{2,3},{3,2},{4,5},{5,4},{6,7},{7,6},{8,9},{9,8},{10,11... | collective-permute-start | bytes 393224 | tf_op jit(solution)/shard_map/ppermute | solution.py:220
  32.5 3.0 %copy-start.2 = (f32[128,256]{1,0:T(8,128)}, f32[128,256]{1,0:T(8,128)S(1)}, u32[]{:S(2)}) copy-start(f32[128,256]{1,0:T(8,128)S(1)} %collective-permute-done.9.refs_6_) | copy-start | bytes 393220
  32.5 2.6 %collective-permute-start.10 = (f32[128,256]{1,0:T(8,128)S(1)}, f32[128,256]{1,0:T(8,128)S(1)}, u32[]{:S(2)}, u32[]{:S(2)}) collective-permute-start(f32[128,256]{1,0:T(8,128)S(1)} %collective-permute-done.9.refs_6_), channel_id=1, source_target_pairs={{0,1},{1,0},{2,3},{3,2},{4,5},{5,4},{6,7},{7,6},{8,9},{9,8},{10,11... | collective-permute-start | bytes 393224 | tf_op jit(solution)/shard_map/ppermute | solution.py:220
  34.0 1.5 %copy-start.3 = (f32[128,256]{1,0:T(8,128)}, f32[128,256]{1,0:T(8,128)S(1)}, u32[]{:S(2)}) copy-start(f32[128,256]{1,0:T(8,128)S(1)} %collective-permute-done.5.refs_2_) | copy-start | bytes 393220
  34.0 1.3 %collective-permute-start.6 = (f32[128,256]{1,0:T(8,128)S(1)}, f32[128,256]{1,0:T(8,128)S(1)}, u32[]{:S(2)}, u32[]{:S(2)}) collective-permute-start(f32[128,256]{1,0:T(8,128)S(1)} %collective-permute-done.5.refs_2_), channel_id=1, source_target_pairs={{0,1},{1,0},{2,3},{3,2},{4,5},{5,4},{6,7},{7,6},{8,9},{9,8},{10,11... | collective-permute-start | bytes 393224 | tf_op jit(solution)/shard_map/ppermute | solution.py:220
  34.0 1.5 %copy-start.4 = (f32[128,256]{1,0:T(8,128)}, f32[128,256]{1,0:T(8,128)S(1)}, u32[]{:S(2)}) copy-start(f32[128,256]{1,0:T(8,128)S(1)} %collective-permute-done.7.refs_4_) | copy-start | bytes 393220
  34.0 1.5 %collective-permute-start.8 = (f32[128,256]{1,0:T(8,128)S(1)}, f32[128,256]{1,0:T(8,128)S(1)}, u32[]{:S(2)}, u32[]{:S(2)}) collective-permute-start(f32[128,256]{1,0:T(8,128)S(1)} %collective-permute-done.7.refs_4_), channel_id=1, source_target_pairs={{0,1},{1,0},{2,3},{3,2},{4,5},{5,4},{6,7},{7,6},{8,9},{9,8},{10,11... | collective-permute-start | bytes 393224 | tf_op jit(solution)/shard_map/ppermute | solution.py:220
  35.2 0.7 copy-start.5
  35.2 0.7 copy-start.6
  35.3 0.6 copy-start.7
  35.5 0.7 copy-start.8
  51.4 10.5 %collective-permute-start.11 = (f32[256,256]{1,0:T(8,128)}, f32[256,256]{1,0:T(8,128)S(1)}, u32[]{:S(2)}, u32[]{:S(2)}) collective-permute-start(f32[256,256]{1,0:T(8,128)} %get-tuple-element.14.own_ref), channel_id=1, source_target_pairs={{0,8},{8,0},{16,24},{24,16},{1,9},{9,1},{17,25},{25,17},{2,10},{10... | collective-permute-start | bytes 786440 | tf_op jit(solution)/shard_map/ppermute | solution.py:220
  61.8 0.7 copy-start.9
  76.1 14.9 %collective-permute-start.12 = (f32[256,256]{1,0:T(8,128)}, f32[256,256]{1,0:T(8,128)S(1)}, u32[]{:S(2)}, u32[]{:S(2)}) collective-permute-start(f32[256,256]{1,0:T(8,128)} %get-tuple-element.16.own_ref), channel_id=1, source_target_pairs={{0,16},{8,24},{16,0},{24,8},{1,17},{9,25},{17,1},{25,9},{2,18},{10... | collective-permute-start | bytes 786440 | tf_op jit(solution)/shard_map/ppermute | solution.py:220
  91.0 0.7 copy-start.10

commit v2 on v1

--- a/solution.py
+++ b/solution.py
@@ -10,6 +10,7 @@
 LEVELS = 2
 TILE = 8
 BLOCK = 64
+LANES = 128
 F32 = jnp.float32
 BF16 = jnp.bfloat16
 EXACT = lax.Precision.HIGHEST
@@ -37,12 +38,6 @@
     )
 
 
-def eye_like(shape):
-    rows = lax.broadcasted_iota(jnp.int32, shape, 0)
-    cols = lax.broadcasted_iota(jnp.int32, shape, 1)
-    return (rows == cols).astype(F32)
-
-
 def over_lanes(tile, lane):
     return jnp.broadcast_to(tile[:, lane : lane + 1], tile.shape)
 
@@ -51,48 +46,90 @@
     return jnp.broadcast_to(tile[row : row + 1, :], tile.shape)
 
 
-def small_inverse_factor(block):
-    n = block.shape[0]
-    wide = jnp.concatenate([block, eye_like((n, n))], axis=1)
-    work = [wide[TILE * t : TILE * (t + 1)] for t in range(n // TILE)]
-    row_of = lax.broadcasted_iota(jnp.int32, work[0].shape, 0)
+def along_lanes(tile, index):
+    return jnp.take_along_axis(tile, index, axis=1, mode="promise_in_bounds")
+
+
+def eliminate(rows, rank, at):
+    count = len(rows)
+    sub = lax.broadcasted_iota(jnp.int32, (TILE, LANES), 0)
+    lane = lax.broadcasted_iota(jnp.int32, (TILE, LANES), 1)
+    inside = (lane >= at) & (lane < at + BLOCK)
+    work = []
+    for t in range(count):
+        unit = (lane == sub + (TILE * t + BLOCK - at)).astype(F32)
+        work.append([jnp.where(inside, rows[t][0], unit)] + list(rows[t][1:]))
     out = []
-    for t in range(len(work)):
-        cols = {u: [over_lanes(work[u], TILE * t + k) for k in range(TILE)] for u in range(t, len(work))}
+    diag = [over_lanes(work[0][0], at + k) for k in range(TILE)]
+    for t in range(count):
+        ahead = None
+        if t + 1 < count:
+            ahead = [over_lanes(work[t + 1][0], at + TILE * (t + 1) + k) for k in range(TILE)]
         pivots = None
         for j in range(TILE):
-            across = [over_rows(cols[t][k], j) if k >= j else None for k in range(TILE)]
-            pivot = across[j]
-            scale = 1.0 / pivot
-            pivot_row = over_rows(work[t], j)
-            pivots = pivot if pivots is None else jnp.where(row_of == j, pivot, pivots)
-            for u in range(t, len(work)):
-                step = cols[u][j] * scale
-                if u == t:
-                    step = jnp.where(row_of > j, step, 0.0)
-                for k in range(j + 1, TILE):
-                    cols[u][k] = cols[u][k] - step * across[k]
-                work[u] = work[u] - step * pivot_row
-        out.append(work[t] * lax.rsqrt(pivots))
-    return jnp.concatenate(out, axis=0)[:, n:]
-
-
-def masked_inverse_factor(gram, rank, s_ref, p_ref):
-    n = gram.shape[0]
-    rows = lax.broadcasted_iota(jnp.int32, (n, n), 0)
-    cols = lax.broadcasted_iota(jnp.int32, (n, n), 1)
-    s_ref[...] = jnp.where((rows < rank) & (cols < rank), gram, (rows == cols).astype(F32))
-    p_ref[...] = (rows == cols).astype(F32)
+            below = [over_rows(diag[k], j) if k >= j else None for k in range(TILE)]
+            pivot = below[j]
+            scale = jnp.where(rank > TILE * t + j, 1.0 / pivot, 0.0)
+            pivots = pivot if pivots is None else jnp.where(sub == j, pivot, pivots)
+            row = [over_rows(part, j) for part in work[t]]
+            scaled = [part * scale for part in row]
+            step = jnp.where(sub > j, diag[j] * scale, 0.0)
+            for k in range(j + 1, TILE):
+                diag[k] = diag[k] - step * below[k]
+            for u in range(t + 1, count):
+                column = along_lanes(row[0], sub + (at + TILE * u))
+                if u == t + 1:
+                    column_scaled = column * scale
+                    for k in range(TILE):
+                        ahead[k] = ahead[k] - column_scaled * over_rows(column, k)
+                work[u] = [part - column * other for part, other in zip(work[u], scaled)]
+            work[t] = [part - step * other for part, other in zip(work[t], row)]
+        root = jnp.where(sub + TILE * t < rank, lax.rsqrt(pivots), 0.0)
+        out.append([part * root for part in work[t]])
+        diag = ahead
+    return out
+
+
+def masked_factor(s_ref, rank, coords_ref, p_ref, own_ref=None):
+    n = s_ref.shape[0]
+    row_of = lax.broadcasted_iota(jnp.int32, (BLOCK, n), 0)
+    col_of = lax.broadcasted_iota(jnp.int32, (BLOCK, n), 1)
+    p_ref[...] = jnp.zeros((n, n), F32)
+    if own_ref is not None:
+        own_ref[...] = jnp.zeros((n, n), F32)
     for low in range(0, n, BLOCK):
         high = low + BLOCK
-        inverse = small_inverse_factor(s_ref[low:high, low:high])
-        extra = contract(inverse, p_ref[low:high, :], 1, 0, EXACT)
-        p_ref[low:high, :] = extra
+        slab = low // LANES * LANES
+        at = low - slab
+        starts = [slab] + ([slab] if at + BLOCK < LANES else []) + list(range(slab + LANES, n, LANES))
+        rows = [[s_ref[r : r + TILE, c : c + LANES] for c in starts] for r in range(low, high, TILE)]
+        out = eliminate(rows, rank - low, at)
+        main = jnp.concatenate([tiles[0] for tiles in out], axis=0)
+        inverse = main[:, BLOCK - at : 2 * BLOCK - at]
+        slabs = {c: jnp.concatenate([tiles[q] for tiles in out], axis=0) for q, c in enumerate(starts)}
+        panel = jnp.concatenate([slabs[c] for c in range(slab, n, LANES)], axis=1)
+        panel = jnp.where(col_of[:, slab:] >= row_of[:, slab:] + low, panel, 0.0)
+        if coords_ref is not None:
+            if slab:
+                coords_ref[low:high, :slab] = jnp.zeros((BLOCK, slab), F32)
+            coords_ref[low:high, slab:] = panel
+        split = halves(panel)
+        if high < n or own_ref is not None:
+            gram = contract3(split, split, 0, 0)
+            if own_ref is not None:
+                own_ref[slab:, slab:] = own_ref[slab:, slab:] + gram
+            if high < n:
+                s_ref[high:, slab:] = s_ref[high:, slab:] - gram[high - slab :, :]
+        if low:
+            p_ref[low:high, :] = contract3(halves(inverse), halves(p_ref[low:high, :]), 1, 0)
+        if at:
+            inverse = jnp.concatenate([jnp.zeros((BLOCK, at), F32), inverse], axis=1)
+            p_ref[low:high, slab:high] = p_ref[low:high, slab:high] + inverse
+        else:
+            p_ref[low:high, low:high] = inverse
         if high < n:
-            panel = contract(inverse, s_ref[low:high, :], 1, 0, EXACT)
-            s_ref[high:, :] = s_ref[high:, :] - contract(panel[:, high:], panel, 0, 0, EXACT)
-            p_ref[high:, :] = p_ref[high:, :] - contract(panel[:, high:], extra, 0, 0, EXACT)
-    p_ref[...] = jnp.where(rows < rank, p_ref[...], 0.0)
+            right = tuple(part[:, high - slab :] for part in split)
+            p_ref[high:, :] = p_ref[high:, :] - contract3(right, halves(p_ref[low:high, :]), 0, 0)
 
 
 def samples_kernel(index_ref, frontal_ref, sketch_ref, out_ref, high_ref, low_ref):
@@ -125,15 +162,9 @@
 
 def leaf_kernel(rank_ref, *refs):
     pieces, (p_ref, coords_ref, own_ref, s_ref) = refs[:-4], refs[-4:]
-    gram = None
-    for piece in pieces:
-        part = halves(piece[...])
-        term = contract3(part, part, 0, 0)
-        gram = term if gram is None else gram + term
-    masked_inverse_factor(gram, rank_ref[0], s_ref, p_ref)
-    coords = contract(p_ref[...], gram, 1, 0, EXACT)
-    coords_ref[...] = coords
-    own_ref[...] = contract(coords, coords, 0, 0, EXACT)
+    samples = halves(jnp.concatenate([piece[...] for piece in pieces], axis=0))
+    s_ref[...] = contract3(samples, samples, 0, 0)
+    masked_factor(s_ref, rank_ref[0], coords_ref, p_ref, own_ref)
 
 
 def leaf_factor(rank, pieces):
@@ -190,27 +221,35 @@
     )(index, inverse, frontal, *pieces)
 
 
+def carried_top(top_ref, coords_ref):
+    return halves(contract3(halves(top_ref[...]), halves(coords_ref[...]), 1, 0))
+
+
 def node_kernel(rank_ref, own_ref, sibling_ref, coords_ref, top_ref, next_own_ref, next_coords_ref, next_top_ref, s_ref, p_ref):
-    pair = own_ref[...] + sibling_ref[...]
-    masked_inverse_factor(pair, rank_ref[0], s_ref, p_ref)
-    inverse = p_ref[...]
-    upper = contract(inverse, pair, 1, 0, EXACT)
-    next_coords_ref[...] = upper
-    next_own_ref[...] = contract(upper, upper, 0, 0, EXACT)
-    carried = contract(top_ref[...], coords_ref[...], 1, 0, EXACT)
-    next_top_ref[...] = contract(carried, inverse, 1, 1, EXACT)
-
-
-def node(rank, own, sibling, coords, top):
+    s_ref[...] = own_ref[...] + sibling_ref[...]
+    carried = carried_top(top_ref, coords_ref)
+    masked_factor(s_ref, rank_ref[0], next_coords_ref, p_ref, next_own_ref)
+    next_top_ref[...] = contract3(carried, halves(p_ref[...]), 1, 1)
+
+
+def last_node_kernel(rank_ref, own_ref, sibling_ref, coords_ref, top_ref, next_top_ref, s_ref, p_ref):
+    s_ref[...] = own_ref[...] + sibling_ref[...]
+    carried = carried_top(top_ref, coords_ref)
+    masked_factor(s_ref, rank_ref[0], None, p_ref)
+    next_top_ref[...] = contract3(carried, halves(p_ref[...]), 1, 1)
+
+
+def node(rank, own, sibling, coords, top, last):
     width = own.shape[0]
     square = jax.ShapeDtypeStruct((width, width), F32)
+    out_shape = (square,) * (0 if last else 2) + (jax.ShapeDtypeStruct(top.shape, F32),)
     return pl.pallas_call(
-        node_kernel,
+        last_node_kernel if last else node_kernel,
         in_specs=[SMEM] + [VMEM] * 4,
-        out_specs=(VMEM,) * 3,
-        out_shape=(square, square, jax.ShapeDtypeStruct(top.shape, F32)),
+        out_specs=(VMEM,) * len(out_shape),
+        out_shape=out_shape,
         scratch_shapes=[pltpu.VMEM((width, width), F32)] * 2,
-        name="node",
+        name="last_node" if last else "node",
     )(rank, own, sibling, coords, top)
 
 
@@ -245,10 +284,10 @@
     sibling = swapped(own, "row", 1)
     leaf_share, coupling = couplings(index, inverse, frontal, pieces)
     top = leaf_share
-    for height in range(1, LEVELS + 1):
-        if height > 1:
-            sibling = swapped(own, "row", 1 << (height - 1))
-        own, coords, top = node(ranks[height], own, sibling, coords, top)
+    for height in range(1, LEVELS):
+        own, coords, top = node(ranks[height], own, sibling, coords, top, False)
+        sibling = swapped(own, "row", 1 << height)
+    (top,) = node(ranks[LEVELS], own, sibling, coords, top, True)
     return (leaf_share, top, coupling)
 
 

time: 105 us -> 90.5 us (0.86)
  Pallas kernels: 63.1 us -> 48.1 us
    pallas_call x2, Pallas kernels: 26.9 us -> 17.4 us  [node(): pl.pallas_call(last_node_kernel if last else node_kernel, in_specs=[SMEM]...]
    pallas_call x1, Pallas kernels: 15.2 us -> 9.74 us  [leaf_factor(): pl.pallas_call(leaf_kernel, in_specs=[SMEM] + [VMEM] * len(pieces), out_s...]
  transfers between devices with their start and end apart: 13 -> 13, of which waited for: 8 -> 8; matrix products, arithmetic and copies ran while one was open for 1% -> 1% of each run, Pallas kernels for 14% -> 17%
where the time goes in v2:
time: 90.5 us; the launch traced here: 90.1 us
  Pallas kernels  48.1 us (53%)
  waiting for transfers between devices  24.6 us (27%)
  starting transfers between devices  12.8 us (14%)
  local copies, waits for them, and re-layouts  2.71 us (3%)
  other arithmetic  1.17 us (1%)
    ppermute x13, waiting for transfers between devices, swapped(): return lax.ppermute(block, axis, route)  24.6 us
    pallas_call x2, Pallas kernels, node(): pl.pallas_call(last_node_kernel if last else node_kernel, in_specs=[SMEM]...  17.4 us
    ppermute x13, starting transfers between devices, swapped(): return lax.ppermute(block, axis, route)  12.8 us
    pallas_call x2, Pallas kernels, partial_samples(): pl.pallas_call(samples_kernel, grid_spec=pltpu.PrefetchScalarGridSpec(num...  12 us
    pallas_call x1, Pallas kernels, leaf_factor(): pl.pallas_call(leaf_kernel, in_specs=[SMEM] + [VMEM] * len(pieces), out_s...  9.74 us
    pallas_call x1, Pallas kernels, couplings(): pl.pallas_call(functools.partial(coupling_kernel, len(pieces)), grid_spec...  8.89 us
    unnamed x22, local copies, waits for them, and re-layouts  2.08 us
  transfers between devices with their start and end apart: 13, of which 8 were waited for; matrix products, arithmetic and copies ran while one was open for 1% of the time, Pallas kernels for 17%

profile of v2, /device:TPU:0, one launch (start us, length us, event | category | flops | bytes accessed | tf_op | source)
XLA Modules:
  0.0 90.1 jit_solution(194807792243087516)
XLA Ops:
  0.6 0.0 copy-start
  0.7 6.0 %partial_samples.3 = f32[512,256]{1,0:T(8,128)} custom-call(s32[1]{0:T(128)} %bitcast.index_ref, f32[1024,2048]{1,0:T(8,128)} %frontal_ref.5, f32[2048,256]{1,0:T(8,128)} %sketch_ref.3), custom_call_target="tpu_custom_call" | custom-call | tf_op jit(solution)/shard_map/partial_samples/pallas_call | solution.py:146
  6.7 0.5 collective-permute-start
  7.2 6.0 %partial_samples.2 = f32[512,256]{1,0:T(8,128)} custom-call(s32[1]{0:T(128)} %bitcast.index_ref, f32[1024,2048]{1,0:T(8,128)} %frontal_ref.5, f32[2048,256]{1,0:T(8,128)} %sketch_ref.3), custom_call_target="tpu_custom_call" | custom-call | tf_op jit(solution)/shard_map/partial_samples/pallas_call | solution.py:146
  13.2 0.0 collective-permute-done
  13.2 1.1 %add.16 = f32[512,256]{1,0:T(8,128)S(1)} add(f32[512,256]{1,0:T(8,128)} %partial_samples.2, f32[512,256]{1,0:T(8,128)S(1)} %collective-permute-done) | non-fusion elementwise | flops 131072 | bytes 1572864 | tf_op jit(solution)/shard_map/add | solution.py:273
  14.3 2.6 %collective-permute-start.1 = (f32[128,256]{1,0:T(8,128)S(1)}, f32[128,256]{1,0:T(8,128)S(1)}, u32[]{:S(2)}, u32[]{:S(2)}) collective-permute-start(f32[128,256]{1,0:T(8,128)S(1)} %get-tuple-element.19), channel_id=1, source_target_pairs={{0,2},{1,3},{2,0},{3,1},{4,6},{5,7},{6,4},{7,5},{8,10},{9,11},{10,... | collective-permute-start | bytes 393224 | tf_op jit(solution)/shard_map/ppermute | solution.py:259
  16.9 1.5 %collective-permute-start.2 = (f32[128,256]{1,0:T(8,128)S(1)}, f32[128,256]{1,0:T(8,128)S(1)}, u32[]{:S(2)}, u32[]{:S(2)}) collective-permute-start(f32[128,256]{1,0:T(8,128)S(1)} %get-tuple-element.21), channel_id=1, source_target_pairs={{0,4},{1,5},{2,6},{3,7},{4,0},{5,1},{6,2},{7,3},{8,12},{9,13},{10,... | collective-permute-start | bytes 393224 | tf_op jit(solution)/shard_map/ppermute | solution.py:259
  18.4 0.0 collective-permute-start.3
  18.4 2.8 %collective-permute-done.1 = f32[128,256]{1,0:T(8,128)S(1)} collective-permute-done((f32[128,256]{1,0:T(8,128)S(1)}, f32[128,256]{1,0:T(8,128)S(1)}, u32[]{:S(2)}, u32[]{:S(2)}) %collective-permute-start.1) | collective-permute-done | bytes 131104 | tf_op jit(solution)/shard_map/ppermute | solution.py:259
  21.2 4.1 %collective-permute-done.2 = f32[128,256]{1,0:T(8,128)S(1)} collective-permute-done((f32[128,256]{1,0:T(8,128)S(1)}, f32[128,256]{1,0:T(8,128)S(1)}, u32[]{:S(2)}, u32[]{:S(2)}) %collective-permute-start.2) | collective-permute-done | bytes 131104 | tf_op jit(solution)/shard_map/ppermute | solution.py:259
  25.3 0.0 collective-permute-done.3
  25.4 0.0 copy-start.1
  25.4 1.6 %collective-permute-start.9 = (f32[128,256]{1,0:T(8,128)S(1)}, f32[128,256]{1,0:T(8,128)S(1)}, u32[]{:S(2)}, u32[]{:S(2)}) collective-permute-start(f32[128,256]{1,0:T(8,128)S(1)} %fusion.1.refs_0_), channel_id=1, source_target_pairs={{0,6},{1,7},{2,4},{3,5},{4,2},{5,3},{6,0},{7,1},{8,14},{9,15},{10,... | collective-permute-start | bytes 393224 | tf_op jit(solution)/shard_map/ppermute | solution.py:259
  26.9 1.5 %collective-permute-start.5 = (f32[128,256]{1,0:T(8,128)S(1)}, f32[128,256]{1,0:T(8,128)S(1)}, u32[]{:S(2)}, u32[]{:S(2)}) collective-permute-start(f32[128,256]{1,0:T(8,128)S(1)} %fusion.1.refs_0_), channel_id=1, source_target_pairs={{0,2},{1,3},{2,0},{3,1},{4,6},{5,7},{6,4},{7,5},{8,10},{9,11},{10,... | collective-permute-start | bytes 393224 | tf_op jit(solution)/shard_map/ppermute | solution.py:259
  28.4 0.5 collective-permute-start.7
  28.9 0.0 collective-permute-start.4
  28.9 3.6 %collective-permute-done.9.refs_6_ = f32[128,256]{1,0:T(8,128)S(1)} collective-permute-done((f32[128,256]{1,0:T(8,128)S(1)}, f32[128,256]{1,0:T(8,128)S(1)}, u32[]{:S(2)}, u32[]{:S(2)}) %collective-permute-start.9) | collective-permute-done | bytes 131104 | tf_op jit(solution)/shard_map/ppermute | solution.py:259
  32.5 0.0 copy-start.2
  32.5 0.0 collective-permute-start.10
  32.5 1.4 %collective-permute-done.5.refs_2_ = f32[128,256]{1,0:T(8,128)S(1)} collective-permute-done((f32[128,256]{1,0:T(8,128)S(1)}, f32[128,256]{1,0:T(8,128)S(1)}, u32[]{:S(2)}, u32[]{:S(2)}) %collective-permute-start.5) | collective-permute-done | bytes 131104 | tf_op jit(solution)/shard_map/ppermute | solution.py:259
  34.0 0.0 copy-start.3
  34.0 0.0 collective-permute-start.6
  34.0 0.1 collective-permute-done.7.refs_4_
  34.0 0.0 copy-start.4
  34.0 0.5 collective-permute-start.8
  34.5 0.0 copy-done
  34.5 0.1 constant_dynamic-slice_fusion
  34.5 0.5 fusion.3
  35.1 0.0 collective-permute-done.4.refs_1_
  35.1 0.0 copy-start.5
  35.1 0.0 collective-permute-done.10.refs_7_
  35.1 0.0 copy-start.6
  35.1 0.2 collective-permute-done.6.refs_3_
  35.3 0.0 copy-start.7
  35.3 0.2 collective-permute-done.8.refs_5_
  35.5 0.0 copy-start.8
  35.5 0.0 copy-done.1
  35.5 0.0 copy-done.2
  35.5 0.0 copy-done.3
  35.5 0.0 copy-done.4
  35.5 0.2 copy-done.5
  35.7 0.1 copy-done.6
  35.8 0.1 copy-done.7
  36.0 0.2 copy-done.8
  36.2 9.7 %leaf_factor.1 = (f32[256,256]{1,0:T(8,128)}, f32[256,256]{1,0:T(8,128)}, f32[256,256]{1,0:T(8,128)}) custom-call(s32[1]{0:T(128)} %bitcast.1.rank_ref, f32[128,256]{1,0:T(8,128)} %copy-done.1, f32[128,256]{1,0:T(8,128)} %copy-done.5, f32[128,256]{1,0:T(8,128)} %copy-done.3, f32[128,256]{1,0:T(8,128)} %copy-done.7, f32[128,256]{1,0:T(8,128)} %copy-done.4, ...), custom_call_target="tpu_custom_call" | custom-call | tf_op jit(solution)/shard_map/leaf_factor/pallas_call | solution.py:173
  45.9 1.6 %collective-permute-start.11 = (f32[256,256]{1,0:T(8,128)}, f32[256,256]{1,0:T(8,128)S(1)}, u32[]{:S(2)}, u32[]{:S(2)}) collective-permute-start(f32[256,256]{1,0:T(8,128)} %get-tuple-element.13.own_ref), channel_id=1, source_target_pairs={{0,8},{8,0},{16,24},{24,16},{1,9},{9,1},{17,25},{25,17},{2,10},{10... | collective-permute-start | bytes 786440 | tf_op jit(solution)/shard_map/ppermute | solution.py:259
  47.5 8.9 %couplings.1 = (f32[128,256]{1,0:T(8,128)}, f32[256,2048]{1,0:T(8,128)}) custom-call(s32[1]{0:T(128)} %bitcast.index_ref, f32[256,256]{1,0:T(8,128)} %get-tuple-element.11.p_ref, f32[1024,2048]{1,0:T(8,128)} %frontal_ref.5, f32[128,256]{1,0:T(8,128)} %copy-done.1, f32[128,256]{1,0:T(8,128)} %copy-done.5, f32[128,256]{1,0:T(8,128)} %copy-done.3, ...), custom_call_target="tpu_custom_call" | custom-call | tf_op jit(solution)/shard_map/couplings/pallas_call | solution.py:203
  56.4 0.0 collective-permute-done.11.sibling_ref
  56.4 0.0 copy-start.9
  56.4 0.7 copy-done.9
  57.1 8.7 %node.1 = (f32[256,256]{1,0:T(8,128)}, f32[256,256]{1,0:T(8,128)}, f32[128,256]{1,0:T(8,128)}) custom-call(s32[1]{0:T(128)} %bitcast.3.rank_ref, f32[256,256]{1,0:T(8,128)} %get-tuple-element.13.own_ref, f32[256,256]{1,0:T(8,128)} %copy-done.9, f32[256,256]{1,0:T(8,128)} %get-tuple-element.14.coords_ref, f32[128,256]{1,0:T(8,128)} %get-tuple-element.8.top_ref), custom_call_target="tpu_custom_call" | custom-call | tf_op jit(solution)/shard_map/node/pallas_call | solution.py:246
  65.8 2.6 %collective-permute-start.12 = (f32[256,256]{1,0:T(8,128)}, f32[256,256]{1,0:T(8,128)S(1)}, u32[]{:S(2)}, u32[]{:S(2)}) collective-permute-start(f32[256,256]{1,0:T(8,128)} %get-tuple-element.15.own_ref), channel_id=1, source_target_pairs={{0,16},{8,24},{16,0},{24,8},{1,17},{9,25},{17,1},{25,9},{2,18},{10... | collective-permute-start | bytes 786440 | tf_op jit(solution)/shard_map/ppermute | solution.py:259
  68.4 12.3 %collective-permute-done.12.sibling_ref = f32[256,256]{1,0:T(8,128)S(1)} collective-permute-done((f32[256,256]{1,0:T(8,128)}, f32[256,256]{1,0:T(8,128)S(1)}, u32[]{:S(2)}, u32[]{:S(2)}) %collective-permute-start.12) | collective-permute-done | bytes 262176 | tf_op jit(solution)/shard_map/ppermute | solution.py:259
  80.6 0.0 copy-start.10
  80.6 0.7 copy-done.10
  81.3 8.7 %last_node.1 = f32[128,256]{1,0:T(8,128)} custom-call(s32[1]{0:T(128)} %bitcast.2.rank_ref, f32[256,256]{1,0:T(8,128)} %get-tuple-element.15.own_ref, f32[256,256]{1,0:T(8,128)} %copy-done.10, f32[256,256]{1,0:T(8,128)} %get-tuple-element.16.coords_ref, f32[128,256]{1,0:T(8,128)} %get-tuple-element.17.top_ref), custom_call_target="tpu_custom_call" | custom-call | tf_op jit(solution)/shard_map/last_node/pallas_call | solution.py:246
  (2 shorter events, 0.1 us)
Async XLA Ops:
  0.6 33.8 %copy-start = (s32[3,4]{1,0:T(4,128)S(1)}, s32[3,4]{1,0:T(4,128)}, u32[]{:S(2)}) copy-start(s32[3,4]{1,0:T(4,128)} %param.5) | copy-start | bytes 148
  6.7 6.5 %collective-permute-start = (f32[512,256]{1,0:T(8,128)}, f32[512,256]{1,0:T(8,128)S(1)}, u32[]{:S(2)}, u32[]{:S(2)}) collective-permute-start(f32[512,256]{1,0:T(8,128)} %partial_samples.3), channel_id=1, source_target_pairs={{0,1},{1,0},{2,3},{3,2},{4,5},{5,4},{6,7},{7,6},{8,9},{9,8},{10,11... | collective-permute-start | bytes 1572872 | tf_op jit(solution)/shard_map/ppermute | solution.py:259
  14.3 6.9 %collective-permute-start.1 = (f32[128,256]{1,0:T(8,128)S(1)}, f32[128,256]{1,0:T(8,128)S(1)}, u32[]{:S(2)}, u32[]{:S(2)}) collective-permute-start(f32[128,256]{1,0:T(8,128)S(1)} %get-tuple-element.19), channel_id=1, source_target_pairs={{0,2},{1,3},{2,0},{3,1},{4,6},{5,7},{6,4},{7,5},{8,10},{9,11},{10,... | collective-permute-start | bytes 393224 | tf_op jit(solution)/shard_map/ppermute | solution.py:259
  16.9 8.4 %collective-permute-start.2 = (f32[128,256]{1,0:T(8,128)S(1)}, f32[128,256]{1,0:T(8,128)S(1)}, u32[]{:S(2)}, u32[]{:S(2)}) collective-permute-start(f32[128,256]{1,0:T(8,128)S(1)} %get-tuple-element.21), channel_id=1, source_target_pairs={{0,4},{1,5},{2,6},{3,7},{4,0},{5,1},{6,2},{7,3},{8,12},{9,13},{10,... | collective-permute-start | bytes 393224 | tf_op jit(solution)/shard_map/ppermute | solution.py:259
  18.4 6.9 %collective-permute-start.3 = (f32[128,256]{1,0:T(8,128)S(1)}, f32[128,256]{1,0:T(8,128)S(1)}, u32[]{:S(2)}, u32[]{:S(2)}) collective-permute-start(f32[128,256]{1,0:T(8,128)S(1)} %get-tuple-element.20), channel_id=1, source_target_pairs={{0,6},{1,7},{2,4},{3,5},{4,2},{5,3},{6,0},{7,1},{8,14},{9,15},{10,... | collective-permute-start | bytes 393224 | tf_op jit(solution)/shard_map/ppermute | solution.py:259
  25.4 10.1 %copy-start.1 = (f32[128,256]{1,0:T(8,128)}, f32[128,256]{1,0:T(8,128)S(1)}, u32[]{:S(2)}) copy-start(f32[128,256]{1,0:T(8,128)S(1)} %fusion.1.refs_0_) | copy-start | bytes 393220
  25.4 7.1 %collective-permute-start.9 = (f32[128,256]{1,0:T(8,128)S(1)}, f32[128,256]{1,0:T(8,128)S(1)}, u32[]{:S(2)}, u32[]{:S(2)}) collective-permute-start(f32[128,256]{1,0:T(8,128)S(1)} %fusion.1.refs_0_), channel_id=1, source_target_pairs={{0,6},{1,7},{2,4},{3,5},{4,2},{5,3},{6,0},{7,1},{8,14},{9,15},{10,... | collective-permute-start | bytes 393224 | tf_op jit(solution)/shard_map/ppermute | solution.py:259
  26.9 7.0 %collective-permute-start.5 = (f32[128,256]{1,0:T(8,128)S(1)}, f32[128,256]{1,0:T(8,128)S(1)}, u32[]{:S(2)}, u32[]{:S(2)}) collective-permute-start(f32[128,256]{1,0:T(8,128)S(1)} %fusion.1.refs_0_), channel_id=1, source_target_pairs={{0,2},{1,3},{2,0},{3,1},{4,6},{5,7},{6,4},{7,5},{8,10},{9,11},{10,... | collective-permute-start | bytes 393224 | tf_op jit(solution)/shard_map/ppermute | solution.py:259
  28.4 5.6 %collective-permute-start.7 = (f32[128,256]{1,0:T(8,128)S(1)}, f32[128,256]{1,0:T(8,128)S(1)}, u32[]{:S(2)}, u32[]{:S(2)}) collective-permute-start(f32[128,256]{1,0:T(8,128)S(1)} %fusion.1.refs_0_), channel_id=1, source_target_pairs={{0,4},{1,5},{2,6},{3,7},{4,0},{5,1},{6,2},{7,3},{8,12},{9,13},{10,... | collective-permute-start | bytes 393224 | tf_op jit(solution)/shard_map/ppermute | solution.py:259
  28.9 6.1 %collective-permute-start.4 = (f32[128,256]{1,0:T(8,128)S(1)}, f32[128,256]{1,0:T(8,128)S(1)}, u32[]{:S(2)}, u32[]{:S(2)}) collective-permute-start(f32[128,256]{1,0:T(8,128)S(1)} %fusion.1.refs_0_), channel_id=1, source_target_pairs={{0,1},{1,0},{2,3},{3,2},{4,5},{5,4},{6,7},{7,6},{8,9},{9,8},{10,11... | collective-permute-start | bytes 393224 | tf_op jit(solution)/shard_map/ppermute | solution.py:259
  32.5 3.0 %copy-start.2 = (f32[128,256]{1,0:T(8,128)}, f32[128,256]{1,0:T(8,128)S(1)}, u32[]{:S(2)}) copy-start(f32[128,256]{1,0:T(8,128)S(1)} %collective-permute-done.9.refs_6_) | copy-start | bytes 393220
  32.5 2.6 %collective-permute-start.10 = (f32[128,256]{1,0:T(8,128)S(1)}, f32[128,256]{1,0:T(8,128)S(1)}, u32[]{:S(2)}, u32[]{:S(2)}) collective-permute-start(f32[128,256]{1,0:T(8,128)S(1)} %collective-permute-done.9.refs_6_), channel_id=1, source_target_pairs={{0,1},{1,0},{2,3},{3,2},{4,5},{5,4},{6,7},{7,6},{8,9},{9,8},{10,11... | collective-permute-start | bytes 393224 | tf_op jit(solution)/shard_map/ppermute | solution.py:259
  34.0 1.5 %copy-start.3 = (f32[128,256]{1,0:T(8,128)}, f32[128,256]{1,0:T(8,128)S(1)}, u32[]{:S(2)}) copy-start(f32[128,256]{1,0:T(8,128)S(1)} %collective-permute-done.5.refs_2_) | copy-start | bytes 393220
  34.0 1.3 %collective-permute-start.6 = (f32[128,256]{1,0:T(8,128)S(1)}, f32[128,256]{1,0:T(8,128)S(1)}, u32[]{:S(2)}, u32[]{:S(2)}) collective-permute-start(f32[128,256]{1,0:T(8,128)S(1)} %collective-permute-done.5.refs_2_), channel_id=1, source_target_pairs={{0,1},{1,0},{2,3},{3,2},{4,5},{5,4},{6,7},{7,6},{8,9},{9,8},{10,11... | collective-permute-start | bytes 393224 | tf_op jit(solution)/shard_map/ppermute | solution.py:259
  34.0 1.5 %copy-start.4 = (f32[128,256]{1,0:T(8,128)}, f32[128,256]{1,0:T(8,128)S(1)}, u32[]{:S(2)}) copy-start(f32[128,256]{1,0:T(8,128)S(1)} %collective-permute-done.7.refs_4_) | copy-start | bytes 393220
  34.0 1.5 %collective-permute-start.8 = (f32[128,256]{1,0:T(8,128)S(1)}, f32[128,256]{1,0:T(8,128)S(1)}, u32[]{:S(2)}, u32[]{:S(2)}) collective-permute-start(f32[128,256]{1,0:T(8,128)S(1)} %collective-permute-done.7.refs_4_), channel_id=1, source_target_pairs={{0,1},{1,0},{2,3},{3,2},{4,5},{5,4},{6,7},{7,6},{8,9},{9,8},{10,11... | collective-permute-start | bytes 393224 | tf_op jit(solution)/shard_map/ppermute | solution.py:259
  35.1 0.7 copy-start.5
  35.1 0.7 copy-start.6
  35.3 0.6 copy-start.7
  35.5 0.7 copy-start.8
  45.9 10.5 %collective-permute-start.11 = (f32[256,256]{1,0:T(8,128)}, f32[256,256]{1,0:T(8,128)S(1)}, u32[]{:S(2)}, u32[]{:S(2)}) collective-permute-start(f32[256,256]{1,0:T(8,128)} %get-tuple-element.13.own_ref), channel_id=1, source_target_pairs={{0,8},{8,0},{16,24},{24,16},{1,9},{9,1},{17,25},{25,17},{2,10},{10... | collective-permute-start | bytes 786440 | tf_op jit(solution)/shard_map/ppermute | solution.py:259
  56.4 0.7 copy-start.9
  65.8 14.9 %collective-permute-start.12 = (f32[256,256]{1,0:T(8,128)}, f32[256,256]{1,0:T(8,128)S(1)}, u32[]{:S(2)}, u32[]{:S(2)}) collective-permute-start(f32[256,256]{1,0:T(8,128)} %get-tuple-element.15.own_ref), channel_id=1, source_target_pairs={{0,16},{8,24},{16,0},{24,8},{1,17},{9,25},{17,1},{25,9},{2,18},{10... | collective-permute-start | bytes 786440 | tf_op jit(solution)/shard_map/ppermute | solution.py:259
  80.6 0.7 copy-start.10
